TPU v7x, 32 devices: a whole 2x2x4 slice. The times are simulated.
32 devices in a mesh: dp: 8 (over y, x, core), tensor: 4 (over z).
Axes of the slice: x: 2, y: 2, z: 4, core: 2. Of those that a mesh axis runs over, the one named last changes fastest.
Arguments:
- block_input: bfloat16 [2048, 2048], P('dp'), may hold values from -6 to 6
- segment_ids: int32 [8, 256], P('dp'), may hold values from 0 to 2, never falling along the last dimension, each value on 1 to 192 neighbouring positions
- expert_ids: int32 [2048, 8], P('dp'), may hold values from 0 to 31, all different within a row; in each aligned block of 256 rows (0 to 255, 256 to 511, ...) at most 128 rows name the same one
- attn_gain: float32 [2048], replicated, may hold values from 0.25 to 1.75
- query_weight: bfloat16 [2048, 4096], P(None, 'tensor'), may hold values from -0.125 to 0.125
- key_projection: bfloat16 [2048, 512], P(None, 'tensor'), may hold values from -0.125 to 0.125
- value_projection: bfloat16 [2048, 512], P(None, 'tensor'), may hold values from -0.125 to 0.125
- query_norm_gain: float32 [128], replicated, may hold values from 0.25 to 1.75
- key_norm_gain: float32 [128], replicated, may hold values from 0.25 to 1.75
- output_projection: bfloat16 [2048, 4096], P(None, 'tensor'), may hold values from -0.375 to 0.375
- ffn_gain: float32 [2048], replicated, may hold values from 0.25 to 1.75
- router_weight: bfloat16 [2048, 32], replicated, may hold values from -0.0625 to 0.0625
- gate_experts: bfloat16 [32, 2048, 768], P('dp', None, 'tensor'), may hold values from -0.125 to 0.125
- up_experts: bfloat16 [32, 2048, 768], P('dp', None, 'tensor'), may hold values from -0.125 to 0.125
- down_experts: bfloat16 [32, 768, 2048], P('dp', 'tensor'), may hold values from -0.4375 to 0.4375
- out_grad: bfloat16 [2048, 2048], P('dp'), may hold values from -6 to 6
Outputs:
- block_output: bfloat16 [2048, 2048], P('dp')
- input_grad: bfloat16 [2048, 2048], P('dp')
- attn_gain_grad: float32 [2048], P('dp')
- query_weight_grad: float32 [2048, 4096], P('dp', 'tensor')
- key_weight_grad: float32 [2048, 512], P('dp', 'tensor')
- value_weight_grad: float32 [2048, 512], P('dp', 'tensor')
- query_gain_grad: float32 [128], P('dp')
- key_gain_grad: float32 [128], P('dp')
- out_weight_grad: float32 [2048, 4096], P('dp', 'tensor')
- ffn_gain_grad: float32 [2048], P('dp')
- router_weight_grad: float32 [2048, 32], P('dp')
- gate_experts_grad: float32 [32, 2048, 768], P('dp', None, 'tensor')
- up_experts_grad: float32 [32, 2048, 768], P('dp', None, 'tensor')
- down_experts_grad: float32 [32, 768, 2048], P('dp', 'tensor')
Inputs may be any that keep to these rules, and one draw needn't show every extreme that they name: `segment_ids`: segment ids never fall along a row; each segment holds 1 to 192 tokens and one of each row holds exactly 192. `expert_ids`: each row names 8 different experts. No expert is named by more than 128 of the rows of one index of dp, a bound that some block reaches by the rows of some index of dp.
All inputs are finite; a program needn't handle non-finite values.
Results may differ from a plain program's by a relative error of at most 0.03.
Values may be sent and summed in bfloat16 or wider, within the bound.
No kernel may reach another device: no remote copies, remote signals or barrier semaphores. Data moves between devices by JAX's collectives and lax.ppermute only.
A program may use at most 320 MiB of HBM per device.

v0:
```python
import jax
import jax.numpy as jnp
from jax import lax
from jax.sharding import PartitionSpec as P

EPS = 1e-06
THETA = 1000000.0
F32 = jnp.float32
BF16 = jnp.bfloat16


def rms_scale(values):
    return lax.rsqrt(jnp.mean(values * values, axis=-1, keepdims=True) + EPS)


def norm_reverse(grad_rows, normed, scale_rows):
    return scale_rows * (grad_rows - normed * jnp.mean(grad_rows * normed, axis=-1, keepdims=True))


def dot_nn(a, b):
    return lax.dot_general(a, b, (((1,), (0,)), ((), ())), preferred_element_type=F32)


def dot_nt(a, b):
    return lax.dot_general(a, b, (((1,), (1,)), ((), ())), preferred_element_type=F32)


def dot_tn(a, b):
    return lax.dot_general(a, b, (((0,), (0,)), ((), ())), preferred_element_type=F32)


def swap(value, bit, count):
    return lax.ppermute(value, "dp", [(i, i ^ bit) for i in range(count)])


def shift(value, step, count):
    return lax.ppermute(value, "tensor", [(i, (i + step) % count) for i in range(count)])


def gather_dp(shard, count):
    if count == 8:
        half = shard.shape[0] // 2
        along_x = swap(shard, 2, count)
        along_y = swap(shard, 4, count)
        mate = swap(shard, 1, count)
        diag_lo = swap(along_y[:half], 2, count)
        diag_hi = swap(along_x[half:], 4, count)
        mate_x = swap(along_x, 1, count)
        mate_y = swap(along_y, 1, count)
        diag = jnp.concatenate([diag_lo, diag_hi], 0)
        mate_d = swap(diag, 1, count)
        return [shard, mate, along_x, mate_x, along_y, mate_y, diag, mate_d]
    return [lax.all_gather(shard, "dp", axis=0, tiled=True)]


def add_b(a, b):
    return (a.astype(F32) + b.astype(F32)).astype(BF16)


def scatter_dp(rows, count):
    if count == 8:
        size = rows.shape[0] // count
        half = size // 2
        chunks = [rows[r * size : (r + 1) * size] for r in range(count)]
        pair = {}
        for r in (6, 4, 2, 0):
            pair[r] = add_b(chunks[r], swap(chunks[r + 1], 1, count))
        from_x = swap(pair[6][:half], 2, count)
        from_y = swap(pair[6][half:], 4, count)
        to_y = jnp.concatenate([add_b(pair[4][:half], from_x), pair[4][half:]], 0)
        to_x = jnp.concatenate([pair[2][:half], add_b(pair[2][half:], from_y)], 0)
        got_x = swap(to_x, 2, count)
        got_y = swap(to_y, 4, count)
        return (pair[0].astype(F32) + got_x.astype(F32) + got_y.astype(F32)).astype(BF16)
    return lax.psum_scatter(rows, "dp", scatter_dimension=0, tiled=True)


def gather_z(shard, count):
    if count == 4:
        half = shard.shape[1] // 2
        prev = shift(shard, 1, count)
        after = shift(shard, -1, count)
        far_lo = shift(prev[:, :half], 1, count)
        far_hi = shift(after[:, half:], -1, count)
        far = jnp.concatenate([far_lo, far_hi], 1)
        return jnp.concatenate([shard, after, far, prev], 0)
    return jnp.concatenate([shard] + [shift(shard, -r, count) for r in range(1, count)], 0)


def scatter_z(rows, count):
    size = rows.shape[0] // count
    block = [rows[r * size : (r + 1) * size] for r in range(count)]
    if count == 4:
        half = rows.shape[1] // 2
        lo = shift(block[2][:, :half], 1, count)
        hi = shift(block[2][:, half:], -1, count)
        up = jnp.concatenate([add_b(block[1][:, :half], lo), block[1][:, half:]], 1)
        down = jnp.concatenate([block[3][:, :half], add_b(block[3][:, half:], hi)], 1)
        got_up = shift(up, 1, count)
        got_down = shift(down, -1, count)
        return block[0].astype(F32) + got_up.astype(F32) + got_down.astype(F32)
    total = block[0].astype(F32)
    for r in range(1, count):
        total = total + shift(block[r], r, count).astype(F32)
    return total


def roll_rows(rows, amount):
    return jnp.roll(rows, amount, axis=0)


def rope_apply(values, cos_rows, sin_rows):
    half = values.shape[-1] // 2
    low, high = (values[..., :half], values[..., half:])
    c, s = (cos_rows[:, None, :], sin_rows[:, None, :])
    return jnp.concatenate([low * c - high * s, high * c + low * s], axis=-1)


def rope_back(values, cos_rows, sin_rows):
    half = values.shape[-1] // 2
    low, high = (values[..., :half], values[..., half:])
    c, s = (cos_rows[:, None, :], sin_rows[:, None, :])
    return jnp.concatenate([low * c + high * s, high * c - low * s], axis=-1)


def local(
    block_input,
    segment_ids,
    expert_ids,
    attn_gain,
    query_weight,
    key_projection,
    value_projection,
    query_norm_gain,
    key_norm_gain,
    output_projection,
    ffn_gain,
    router_weight,
    gate_experts,
    up_experts,
    down_experts,
    out_grad,
):
    tokens, width = block_input.shape
    head_dim = query_norm_gain.shape[0]
    experts_dev, _, hidden_dev = gate_experts.shape
    n_dp = lax.axis_size("dp")
    n_t = lax.axis_size("tensor")
    num_experts = experts_dev * n_dp
    part = tokens // n_t
    flat = experts_dev * hidden_dev
    t_index = lax.axis_index("tensor")
    d_index = lax.axis_index("dp")
    turn = t_index * part
    scale_value = head_dim ** (-0.5)
    x_rows = roll_rows(block_input, -turn)
    seg = roll_rows(segment_ids[0], -turn)
    ids = roll_rows(expert_ids, -turn)
    dy_rows = roll_rows(out_grad, -turn)
    order = (jnp.arange(tokens, dtype=jnp.int32) + turn) % tokens
    dy_chunks = gather_dp(dy_rows, n_dp)
    ids_all = jnp.concatenate(gather_dp(ids, n_dp), 0)
    dy_all = jnp.concatenate(dy_chunks, 0)
    inputs_f = x_rows.astype(F32)
    scale_one = rms_scale(inputs_f)
    normed_one = inputs_f * scale_one
    attn_in = (normed_one * attn_gain).astype(BF16)
    same = seg[:, None] == seg[None, :]
    earlier = order[None, :] < order[:, None]
    positions = jnp.sum((same & earlier).astype(jnp.int32), axis=1)
    half_dim = head_dim // 2
    frequency = THETA ** (-(jnp.arange(half_dim, dtype=F32) * 2.0) / head_dim)
    angles = positions.astype(F32)[:, None] * frequency[None, :]
    cos_rows, sin_rows = (jnp.cos(angles), jnp.sin(angles))
    allowed = same & (order[None, :] <= order[:, None])
    q_raw = dot_nn(attn_in, query_weight).reshape(tokens, -1, head_dim)
    q_scale = rms_scale(q_raw)
    q_hat = q_raw * q_scale
    k_raw = dot_nn(attn_in, key_projection).reshape(tokens, -1, head_dim)
    k_scale = rms_scale(k_raw)
    k_hat = k_raw * k_scale
    k_rot = rope_apply(k_hat * key_norm_gain, cos_rows, sin_rows).astype(BF16)
    v_rows = dot_nn(attn_in, value_projection).astype(BF16).reshape(tokens, -1, head_dim)
    heads = q_raw.shape[1]
    kv = k_raw.shape[1]
    group = heads // kv
    q_rot = rope_apply(q_hat * query_norm_gain, cos_rows, sin_rows).astype(BF16)
    q_rot = q_rot.reshape(tokens, kv, group, head_dim)
    scores = jnp.einsum("qkgd,skd->kgqs", q_rot, k_rot, preferred_element_type=F32) * scale_value
    scores = jnp.where(allowed, scores, -jnp.inf)
    top = jnp.max(scores, axis=-1, keepdims=True)
    weights = jnp.exp(scores - top)
    totals = jnp.sum(weights, axis=-1, keepdims=True)
    probs = weights / totals
    probs_b = probs.astype(BF16)
    attn_out = jnp.einsum("kgqs,skd->qkgd", probs_b, v_rows, preferred_element_type=F32)
    attn_out = attn_out.astype(BF16)
    attn_flat = attn_out.reshape(tokens, heads * head_dim)
    attn_part = dot_nt(attn_flat, output_projection).astype(BF16)
    attn_sum = scatter_z(attn_part, n_t)
    x_own = inputs_f[:part]
    ids_own = ids[:part]
    middle = x_own + attn_sum
    scale_two = rms_scale(middle)
    normed_two = middle * scale_two
    ffn_own = (normed_two * ffn_gain).astype(BF16)
    ffn_rows = gather_z(ffn_own, n_t)
    x_all = jnp.concatenate(gather_dp(ffn_rows, n_dp), 0)

    def router(rows, chosen):
        logits = dot_nn(rows, router_weight)
        raised = jnp.exp(logits - jnp.max(logits, axis=-1, keepdims=True))
        prob = raised / jnp.sum(raised, axis=-1, keepdims=True)
        names = jnp.arange(num_experts, dtype=jnp.int32)
        mask = jnp.any(chosen[:, :, None] == names[None, None, :], axis=1).astype(F32)
        total = jnp.sum(prob * mask, axis=-1, keepdims=True)
        return (prob, mask, total, prob * mask / total)

    prob_own, mask_own, total_own, gate_own = router(ffn_own, ids_own)
    gate_all = router(x_all, ids_all)[3]
    owner = d_index * experts_dev + jnp.arange(flat, dtype=jnp.int32) // hidden_dev
    names = jnp.arange(num_experts, dtype=jnp.int32)
    place = (names[:, None] == owner[None, :]).astype(F32)
    gate_wide = jnp.dot(gate_all, place, precision=lax.Precision.HIGHEST)
    wg = jnp.transpose(gate_experts, (0, 2, 1)).reshape(flat, width)
    wu = jnp.transpose(up_experts, (0, 2, 1)).reshape(flat, width)
    wd = down_experts.reshape(flat, width)
    d_hidden = dot_nt(dy_all, wd)
    gate_pre = dot_nt(x_all, wg)
    up_pre = dot_nt(x_all, wu)
    sig = jax.nn.sigmoid(gate_pre)
    act = gate_pre * sig
    hidden = act * up_pre
    hidden_g = (hidden * gate_wide).astype(BF16)
    gate_grads = lax.dot_general(
        hidden * d_hidden, place, (((1,), (1,)), ((), ())), precision=lax.Precision.HIGHEST
    )
    hidden_grad = d_hidden * gate_wide
    dg = (hidden_grad * up_pre * sig * (1.0 + gate_pre * (1.0 - sig))).astype(BF16)
    du = (hidden_grad * act).astype(BF16)
    back = (dot_nn(dg, wg) + dot_nn(du, wu)).astype(BF16)
    pad = -num_experts % 128
    back = jnp.concatenate([back, jnp.pad(gate_grads, ((0, 0), (0, pad))).astype(BF16)], 1)
    back_sum = scatter_dp(back, n_dp)
    back_own = scatter_z(back_sum, n_t)
    ffn_back = back_own[:, :width]
    gate_grad = back_own[:, width : width + num_experts]
    mix = dot_nn(hidden_g, wd).astype(BF16)
    mix_sum = scatter_dp(mix, n_dp)
    mix_own = scatter_z(mix_sum, n_t)
    block_out = gather_z((middle + mix_own).astype(BF16), n_t)
    block_output = roll_rows(block_out, turn)
    down_grad = dot_tn(hidden_g, dy_all).reshape(experts_dev, hidden_dev, width)
    gate_w_grad = dot_tn(dg, x_all).reshape(experts_dev, hidden_dev, width).transpose(0, 2, 1)
    up_w_grad = dot_tn(du, x_all).reshape(experts_dev, hidden_dev, width).transpose(0, 2, 1)
    select_grad = (gate_grad - jnp.sum(gate_grad * gate_own, axis=-1, keepdims=True)) / total_own
    prob_grad = mask_own * select_grad
    logit_grad = (
        prob_own * (prob_grad - jnp.sum(prob_grad * prob_own, axis=-1, keepdims=True))
    ).astype(BF16)
    router_part = dot_tn(ffn_own, logit_grad)
    ffn_grad = ffn_back + dot_nt(logit_grad, router_weight)
    ffn_gain_part = jnp.sum(ffn_grad * normed_two, axis=0)
    mid_grad = dy_rows[:part].astype(F32) + norm_reverse(ffn_grad * ffn_gain, normed_two, scale_two)
    mid_rows = gather_z(mid_grad.astype(BF16), n_t)
    d_attn = dot_nn(mid_rows, output_projection).astype(BF16)
    d_out = d_attn.reshape(tokens, kv, group, head_dim)
    delta = jnp.sum(d_out.astype(F32) * attn_out.astype(F32), axis=-1)
    delta = jnp.transpose(delta, (1, 2, 0))[..., None]
    v_grad = jnp.einsum("kgqs,qkgd->skd", probs_b, d_out, preferred_element_type=F32)
    p_grad = jnp.einsum("qkgd,skd->kgqs", d_out, v_rows, preferred_element_type=F32)
    s_grad = (probs * (p_grad - delta) * scale_value).astype(BF16)
    q_grad = jnp.einsum("kgqs,skd->qkgd", s_grad, k_rot, preferred_element_type=F32)
    k_grad = jnp.einsum("kgqs,qkgd->skd", s_grad, q_rot, preferred_element_type=F32)
    q_back = rope_back(q_grad.reshape(tokens, heads, head_dim), cos_rows, sin_rows)
    q_gain_part = jnp.sum(q_back * q_hat, axis=(0, 1))
    q_raw_grad = norm_reverse(q_back * query_norm_gain, q_hat, q_scale).astype(BF16)
    q_raw_grad = q_raw_grad.reshape(tokens, -1)
    k_back = rope_back(k_grad, cos_rows, sin_rows)
    k_gain_part = jnp.sum(k_back * k_hat, axis=(0, 1))
    k_raw_grad = norm_reverse(k_back * key_norm_gain, k_hat, k_scale).astype(BF16)
    k_raw_grad = k_raw_grad.reshape(tokens, -1)
    v_grad_b = v_grad.astype(BF16).reshape(tokens, -1)
    in_part = (
        dot_nt(q_raw_grad, query_weight)
        + dot_nt(k_raw_grad, key_projection)
        + dot_nt(v_grad_b, value_projection)
    ).astype(BF16)
    attn_in_grad = scatter_z(in_part, n_t)
    normed_own = normed_one[:part]
    attn_gain_part = jnp.sum(attn_in_grad * normed_own, axis=0)
    input_own = mid_grad + norm_reverse(attn_in_grad * attn_gain, normed_own, scale_one[:part])
    input_grad = roll_rows(gather_z(input_own.astype(BF16), n_t), turn)

    def weight_grad(rows_dp, columns_dp):
        return dot_tn(jnp.concatenate(rows_dp, 0), jnp.concatenate(columns_dp, 0))

    slab = width // n_dp

    def spread(rows):
        if n_dp != 8:
            return [lax.all_to_all(rows, "dp", split_axis=1, concat_axis=0, tiled=True)]
        out = []
        for r in range(n_dp):
            piece = lax.dynamic_slice_in_dim(rows, (d_index ^ r) * slab, slab, 1)
            out.append(piece if r == 0 else swap(piece, r, n_dp))
        return out

    attn_in_slab = spread(attn_in)
    mid_slab = spread(mid_rows)
    out_weight_grad = weight_grad(mid_slab, gather_dp(attn_flat, n_dp))
    qkv_grad = jnp.concatenate([q_raw_grad, k_raw_grad, v_grad_b], 1)
    qkv_w = weight_grad(attn_in_slab, gather_dp(qkv_grad, n_dp))
    q_cols = heads * head_dim
    kv_cols = kv * head_dim
    query_weight_grad = qkv_w[:, :q_cols]
    key_weight_grad = qkv_w[:, q_cols : q_cols + kv_cols]
    value_weight_grad = qkv_w[:, q_cols + kv_cols :]
    router_sum = lax.psum(
        lax.psum_scatter(router_part.astype(BF16), "dp", scatter_dimension=0, tiled=True), "tensor"
    ).astype(F32)
    gains = jnp.concatenate([attn_gain_part, ffn_gain_part, q_gain_part, k_gain_part])
    gains = lax.psum(gains, ("dp", "tensor"))

    def mine(vector):
        size = vector.shape[0] // n_dp
        return lax.dynamic_slice_in_dim(vector, d_index * size, size, 0)

    return (
        block_output,
        input_grad,
        mine(gains[:width]),
        query_weight_grad,
        key_weight_grad,
        value_weight_grad,
        mine(gains[2 * width : 2 * width + head_dim]),
        mine(gains[2 * width + head_dim :]),
        out_weight_grad,
        mine(gains[width : 2 * width]),
        router_sum,
        gate_w_grad,
        up_w_grad,
        down_grad,
    )


def solution(mesh):
    return jax.shard_map(
        local,
        mesh=mesh,
        in_specs=(
            P("dp", None),
            P("dp", None),
            P("dp", None),
            P(),
            P(None, "tensor"),
            P(None, "tensor"),
            P(None, "tensor"),
            P(),
            P(),
            P(None, "tensor"),
            P(),
            P(),
            P("dp", None, "tensor"),
            P("dp", None, "tensor"),
            P("dp", "tensor", None),
            P("dp", None),
        ),
        out_specs=(
            P("dp", None),
            P("dp", None),
            P("dp"),
            P("dp", "tensor"),
            P("dp", "tensor"),
            P("dp", "tensor"),
            P("dp"),
            P("dp"),
            P("dp", "tensor"),
            P("dp"),
            P("dp", None),
            P("dp", None, "tensor"),
            P("dp", None, "tensor"),
            P("dp", "tensor", None),
        ),
        check_vma=False,
    )
```

profile of v0, /device:TPU:0, one launch (start us, length us, event | category | flops | bytes accessed | tf_op | source)
XLA Modules:
  0.0 638.1 jit_solution(17216061805389194970)
XLA Ops:
  75.1 4.1 collective-permute-done.76
  83.7 6.4 %collective-permute-done.1 = bf16[64,2048]{1,0:T(8,128)(2,1)S(1)} collective-permute-done((bf16[64,2048]{1,0:T(8,128)(2,1)S(1)}, bf16[64,2048]{1,0:T(8,128)(2,1)S(1)}, u32[]{:S(2)}, u32[]{:S(2)}) %collective-permute-start.1) | collective-permute-done | bytes 262176 | tf_op jit(solution)/shard_map/ppermute | solution.py:37
  121.8 9.1 %collective-permute-done.43 = bf16[256,2048]{1,0:T(8,128)(2,1)S(1)} collective-permute-done((bf16[256,2048]{1,0:T(8,128)(2,1)S(1)}, bf16[256,2048]{1,0:T(8,128)(2,1)S(1)}, u32[]{:S(2)}, u32[]{:S(2)}) %collective-permute-start.43) | collective-permute-done | bytes 1048608 | tf_op jit(solution)/shard_map/ppermute | solution.py:33
  144.5 25.2 %collective-permute-done.45 = bf16[128,2048]{1,0:T(8,128)(2,1)S(1)} collective-permute-done((bf16[128,2048]{1,0:T(8,128)(2,1)S(1)}, bf16[128,2048]{1,0:T(8,128)(2,1)S(1)}, u32[]{:S(2)}, u32[]{:S(2)}) %collective-permute-start.45) | collective-permute-done | bytes 524320 | tf_op jit(solution)/shard_map/ppermute | solution.py:33
  181.9 5.3 collective-permute-done.13
  189.9 9.1 %fusion.111 = f32[2048,768]{1,0:T(8,128)S(1)} fusion(bf16[2048,2048]{1,0:T(8,128)(2,1)} %constant_dynamic-update-slice_fusion.21, bf16[768,2048]{1,0:T(8,128)(2,1)S(1)} %bitcast.211), kind=kOutput, calls=%fused_computation.348 | convolution fusion | flops 6442450944 | bytes 17825792 | tf_op jit(solution)/shard_map/dot_general | solution.py:25
  204.4 8.6 %fusion.110 = f32[2048,768]{1,0:T(8,128)} fusion(bf16[2048,2048]{1,0:T(8,128)(2,1)S(1)} %constant_dynamic-update-slice_fusion, bf16[768,2048]{1,0:T(8,128)(2,1)S(1)} %bitcast.209), kind=kOutput, calls=%fused_computation.347 | convolution fusion | flops 6442450944 | bytes 17825792 | tf_op jit(solution)/shard_map/dot_general | solution.py:25
  213.0 8.6 %fusion.109 = f32[2048,768]{1,0:T(8,128)} fusion(bf16[2048,2048]{1,0:T(8,128)(2,1)S(1)} %constant_dynamic-update-slice_fusion, bf16[768,2048]{1,0:T(8,128)(2,1)S(1)} %bitcast.192), kind=kOutput, calls=%fused_computation.346 | convolution fusion | flops 6442450944 | bytes 17825792 | tf_op jit(solution)/shard_map/dot_general | solution.py:25
  221.6 7.6 %fusion.7 = bf16[2048,32]{0,1:T(8,128)(2,1)} fusion(f32[2048,768]{1,0:T(8,128)S(1)} %fusion.111, f32[2048,768]{1,0:T(8,128)S(1)} %copy-done.106, s32[768]{0:T(1024)S(1)} %fusion.79, f32[2048,768]{1,0:T(8,128)} %fusion.109), kind=kOutput, calls=%fused_computation.17 | convolution fusion | flops 613507072 | bytes 19008512 | tf_op jit(solution)/shard_map/dot_general | solution.py:235
  231.2 10.7 %multiply_convert_fusion = (bf16[2048,768]{1,0:T(8,128)(2,1)S(1)}, bf16[2048,768]{1,0:T(8,128)(2,1)S(1)}, bf16[2048,768]{1,0:T(8,128)(2,1)}) fusion(f32[2048,768]{1,0:T(8,128)} %copy-done.105, f32[2048,768]{1,0:T(8,128)} %fusion.109, f32[2048,768]{1,0:T(8,128)} %fusion.110, s32[768]{0:T(1024)S(1)} %fusion.79, f32[2048]{0:T(1024)S(1)} %fusion.76, ...), kind=kOutput, calls=%fused_computation.7 | convolution fusion | flops 631005184 | bytes 28666880 | tf_op jit(solution)/shard_map/dot_general | solution.py:224
  242.0 9.5 %fusion.112 = f32[2048,2048]{1,0:T(8,128)} fusion(bf16[2048,768]{1,0:T(8,128)(2,1)S(1)} %get-tuple-element.34, bf16[768,2048]{1,0:T(8,128)(2,1)S(1)} %bitcast.193), kind=kOutput, calls=%fused_computation.349 | convolution fusion | flops 6442450944 | bytes 23068672 | tf_op jit(solution)/shard_map/dot_general | solution.py:21
  251.5 12.6 %add_convert_fusion = bf16[2048,2048]{1,0:T(8,128)(2,1)} fusion(f32[2048,2048]{1,0:T(8,128)} %fusion.112, bf16[2048,768]{1,0:T(8,128)(2,1)S(1)} %get-tuple-element.33, bf16[768,2048]{1,0:T(8,128)(2,1)S(1)} %bitcast.210), kind=kOutput, calls=%fused_computation.2 | convolution fusion | flops 6450839552 | bytes 31457280 | tf_op jit(solution)/shard_map/dot_general | solution.py:21
  264.0 8.0 %fusion.1 = bf16[2048,2176]{1,0:T(8,128)(2,1)} fusion(bf16[2048,32]{1,0:T(8,128)(2,1)S(1)} %copy-done.26, bf16[2048,2048]{1,0:T(8,128)(2,1)} %add_convert_fusion), kind=kLoop, calls=%fused_computation.3 | loop fusion | flops 26738688 | bytes 17432576 | tf_op jit(solution)/shard_map/concatenate | solution.py:243
  272.0 4.2 fusion.94
  276.7 9.2 %convolution_convert_fusion = bf16[2048,2048]{1,0:T(8,128)(2,1)S(1)} fusion(bf16[2048,768]{1,0:T(8,128)(2,1)} %get-tuple-element.35, bf16[768,2048]{1,0:T(8,128)(2,1)S(1)} %bitcast.212), kind=kOutput, calls=%fused_computation.4 | convolution fusion | flops 6446645248 | bytes 14680064 | tf_op jit(solution)/shard_map/dot_general | solution.py:21
  288.4 10.5 %fusion.116 = f32[768,2048]{1,0:T(8,128)} fusion(bf16[2048,768]{1,0:T(8,128)(2,1)} %copy-done.109, bf16[2048,2048]{1,0:T(8,128)(2,1)S(1)} %bitcast.200), kind=kOutput, calls=%fused_computation.353 | convolution fusion | flops 6442450944 | bytes 17825792 | tf_op jit(solution)/shard_map/dot_general | solution.py:29
  310.9 8.4 %collective-permute-done.30 = bf16[128,2048]{1,0:T(8,128)(2,1)} collective-permute-done((bf16[128,2048]{1,0:T(8,128)(2,1)}, bf16[128,2048]{1,0:T(8,128)(2,1)}, u32[]{:S(2)}, u32[]{:S(2)}) %collective-permute-start.30) | collective-permute-done | bytes 524320 | tf_op jit(solution)/shard_map/ppermute | solution.py:33
  323.0 7.7 %collective-permute-done.54 = bf16[128,2176]{1,0:T(8,128)(2,1)S(1)} collective-permute-done((bf16[128,2176]{1,0:T(8,128)(2,1)S(1)}, bf16[128,2176]{1,0:T(8,128)(2,1)S(1)}, u32[]{:S(2)}, u32[]{:S(2)}) %collective-permute-start.54) | collective-permute-done | bytes 557088 | tf_op jit(solution)/shard_map/ppermute | solution.py:33
  337.4 10.7 %fusion.117 = f32[768,2048]{1,0:T(8,128)} fusion(bf16[2048,768]{1,0:T(8,128)(2,1)} %copy-done.108, bf16[2048,2048]{1,0:T(8,128)(2,1)S(1)} %bitcast.200), kind=kOutput, calls=%fused_computation.354 | convolution fusion | flops 6442450944 | bytes 17825792 | tf_op jit(solution)/shard_map/dot_general | solution.py:29
  348.1 9.2 %collective-permute-done.31 = bf16[256,2048]{1,0:T(8,128)(2,1)S(1)} collective-permute-done((bf16[256,2048]{1,0:T(8,128)(2,1)S(1)}, bf16[256,2048]{1,0:T(8,128)(2,1)S(1)}, u32[]{:S(2)}, u32[]{:S(2)}) %collective-permute-start.31) | collective-permute-done | bytes 1048608 | tf_op jit(solution)/shard_map/ppermute | solution.py:33
  359.3 20.0 %collective-permute-done.55 = bf16[256,2176]{1,0:T(8,128)(2,1)S(1)} collective-permute-done((bf16[256,2176]{1,0:T(8,128)(2,1)S(1)}, bf16[256,2176]{1,0:T(8,128)(2,1)S(1)}, u32[]{:S(2)}, u32[]{:S(2)}) %collective-permute-start.55) | collective-permute-done | bytes 1114144 | tf_op jit(solution)/shard_map/ppermute | solution.py:33
  395.1 11.0 %fusion.118 = f32[768,2048]{1,0:T(8,128)} fusion(bf16[2048,768]{1,0:T(8,128)(2,1)S(1)} %copy-done.107, bf16[2048,2048]{1,0:T(8,128)(2,1)} %constant_dynamic-update-slice_fusion.21), kind=kOutput, calls=%fused_computation.355 | convolution fusion | flops 6442450944 | bytes 17825792 | tf_op jit(solution)/shard_map/dot_general | solution.py:29
  416.8 7.9 %collective-permute-done.60 = bf16[64,2048]{1,0:T(8,128)(2,1)S(1)} collective-permute-done((bf16[64,2048]{1,0:T(8,128)(2,1)S(1)}, bf16[64,2048]{1,0:T(8,128)(2,1)S(1)}, u32[]{:S(2)}, u32[]{:S(2)}) %collective-permute-start.60) | collective-permute-done | bytes 262176 | tf_op jit(solution)/shard_map/ppermute | solution.py:37
  428.1 4.8 collective-permute-start.62
  433.6 15.8 %reduce-scatter.2.cloned.1.call-done = bf16[256,32]{0,1:T(8,128)(2,1)} async-done(((bf16[2048,32]{0,1:T(8,128)(2,1)}), bf16[256,32]{0,1:T(8,128)(2,1)}) %reduce-scatter.2.cloned.1.call-update) | async-done | bytes 16400 | tf_op jit(solution)/shard_map/reduce_scatter | solution.py:320
  449.4 19.5 %psum.15 = bf16[256,32]{0,1:T(8,128)(2,1)S(1)} all-reduce(bf16[256,32]{0,1:T(8,128)(2,1)} %reduce-scatter.2.cloned.1.call-done), channel_id=1, replica_groups=mesh['dp'=8,'tensor'=4] {'tensor'}, use_global_device_ids=true, to_apply=%region_29.31 | all-reduce | flops 8192 | bytes 32768 | tf_op jit(solution)/shard_map/psum | solution.py:319
  509.5 5.9 collective-permute-start.67
  516.8 5.0 collective-permute-done.67
  539.3 39.3 %psum.14 = f32[4352]{0:T(1024)S(1)} all-reduce(f32[4352]{0:T(1024)S(1)} %pad_maximum_fusion.24), channel_id=1, replica_groups=mesh['dp'=8,'tensor'=4] {'dp','tensor'}, use_global_device_ids=true, to_apply=%region_27.29 | all-reduce | flops 4352 | bytes 34816 | tf_op jit(solution)/shard_map/psum | solution.py:323
  583.2 10.7 %collective-permute-done.69 = bf16[64,2048]{1,0:T(8,128)(2,1)S(1)} collective-permute-done((bf16[64,2048]{1,0:T(8,128)(2,1)S(1)}, bf16[64,2048]{1,0:T(8,128)(2,1)S(1)}, u32[]{:S(2)}, u32[]{:S(2)}) %collective-permute-start.69) | collective-permute-done | bytes 262176 | tf_op jit(solution)/shard_map/ppermute | solution.py:37
  610.8 7.6 %fusion.33 = bf16[256,2048]{1,0:T(8,128)(2,1)} fusion(s32[]{:T(128)S(6)} %select_n.114, bf16[64,2048]{1,0:T(8,128)(2,1)} %get-tuple-element.107, bf16[64,2048]{1,0:T(8,128)(2,1)S(1)} %collective-permute-done.36, bf16[64,1024]{1,0:T(8,128)(2,1)S(1)} %collective-permute-done.38, bf16[64,1024]{1,0:T(8,128)(2,1)S(1)} %collective-permute-done.39, ...), kind=kLoop, calls=%fused_computation.92 | loop fusion | flops 10485760 | bytes 2097156 | tf_op jit(solution)/shard_map/jit(_roll_dynamic)/concatenate | solution.py:109
  618.6 6.5 %fusion.23 = bf16[256,2048]{1,0:T(8,128)(2,1)} fusion(s32[]{:T(128)S(6)} %select_n.114, bf16[64,2048]{1,0:T(8,128)(2,1)S(1)} %get-tuple-element.106, bf16[64,2048]{1,0:T(8,128)(2,1)S(1)} %collective-permute-done.68, bf16[64,1024]{1,0:T(8,128)(2,1)S(1)} %collective-permute-done.70, bf16[64,1024]{1,0:T(8,128)(2,1)S(1)} %collective-permute-done.71, ...), kind=kLoop, calls=%fused_computation.82 | loop fusion | flops 10485760 | bytes 2097156 | tf_op jit(solution)/shard_map/jit(_roll_dynamic)/concatenate | solution.py:109
  (648 shorter events, 282.4 us)
Async XLA Ops:
  7.2 442.2 %reduce-scatter.2.cloned.1.call-start = ((), (), s32[]{:S(2)}) async-start(), calls=%async_computation.1 | async-start | bytes 147456 | tf_op jit(solution)/shard_map/reduce_scatter | solution.py:320
  8.8 44.6 %collective-permute-start.16 = (s32[256,8]{0,1:T(8,128)S(1)}, s32[256,8]{0,1:T(8,128)S(1)}, u32[]{:S(2)}, u32[]{:S(2)}) collective-permute-start(s32[256,8]{0,1:T(8,128)S(1)} %get-tuple-element.28), channel_id=1, source_target_pairs={{0,4},{4,0},{8,12},{12,8},{16,20},{20,16},{24,28},{28,24},{1,5},{5... | collective-permute-start | bytes 24584 | tf_op jit(solution)/shard_map/ppermute | solution.py:33
  9.3 43.6 %collective-permute-start.17 = (s32[256,8]{0,1:T(8,128)S(1)}, s32[256,8]{0,1:T(8,128)S(1)}, u32[]{:S(2)}, u32[]{:S(2)}) collective-permute-start(s32[256,8]{0,1:T(8,128)S(1)} %get-tuple-element.28), channel_id=1, source_target_pairs={{0,8},{4,12},{8,0},{12,4},{16,24},{20,28},{24,16},{28,20},{1,9},{5... | collective-permute-start | bytes 24584 | tf_op jit(solution)/shard_map/ppermute | solution.py:33
  11.8 38.7 %collective-permute-start.19 = (s32[256,8]{0,1:T(8,128)S(1)}, s32[256,8]{0,1:T(8,128)S(1)}, u32[]{:S(2)}, u32[]{:S(2)}) collective-permute-start(s32[256,8]{0,1:T(8,128)S(1)} %get-tuple-element.28), channel_id=1, source_target_pairs={{0,16},{4,20},{8,24},{12,28},{16,0},{20,4},{24,8},{28,12},{1,17},{... | collective-permute-start | bytes 24584 | tf_op jit(solution)/shard_map/ppermute | solution.py:33
  31.7 68.2 %collective-permute-start.94 = (bf16[256,1024]{0,1:T(8,128)(2,1)}, bf16[256,1024]{0,1:T(8,128)(2,1)}, u32[]{:S(2)}, u32[]{:S(2)}) collective-permute-start(bf16[256,1024]{0,1:T(8,128)(2,1)} %bitcast.11), channel_id=1, source_target_pairs={{0,4},{4,0},{8,12},{12,8},{16,20},{20,16},{24,28},{28,24},{1,5},{5... | collective-permute-start | bytes 1572872 | tf_op jit(solution)/shard_map/ppermute | solution.py:33
  37.2 27.6 %collective-permute-start = (bf16[64,1024]{1,0:T(8,128)(2,1)}, bf16[64,1024]{1,0:T(8,128)(2,1)}, u32[]{:S(2)}, u32[]{:S(2)}) collective-permute-start(bf16[64,1024]{1,0:T(8,128)(2,1)} %get-tuple-element.100), channel_id=1, source_target_pairs={{0,1},{1,2},{2,3},{3,0},{4,5},{5,6},{6,7},{7,4},{8,9},{9,10},{10,1... | collective-permute-start | bytes 393224 | tf_op jit(solution)/shard_map/ppermute | solution.py:37
  96.8 34.2 %collective-permute-start.40 = (bf16[256,2048]{1,0:T(8,128)(2,1)}, bf16[256,2048]{1,0:T(8,128)(2,1)S(1)}, u32[]{:S(2)}, u32[]{:S(2)}) collective-permute-start(bf16[256,2048]{1,0:T(8,128)(2,1)} %get-tuple-element.22), channel_id=1, source_target_pairs={{0,4},{4,0},{8,12},{12,8},{16,20},{20,16},{24,28},{28,24},{1,5},{5... | collective-permute-start | bytes 3145736 | tf_op jit(solution)/shard_map/ppermute | solution.py:33
  106.4 24.5 %collective-permute-start.43 = (bf16[256,2048]{1,0:T(8,128)(2,1)S(1)}, bf16[256,2048]{1,0:T(8,128)(2,1)S(1)}, u32[]{:S(2)}, u32[]{:S(2)}) collective-permute-start(bf16[256,2048]{1,0:T(8,128)(2,1)S(1)} %copy-done.21), channel_id=1, source_target_pairs={{0,16},{4,20},{8,24},{12,28},{16,0},{20,4},{24,8},{28,12},{1,17},{... | collective-permute-start | bytes 3145736 | tf_op jit(solution)/shard_map/ppermute | solution.py:33
  111.7 23.8 %collective-permute-start.41 = (bf16[256,2048]{1,0:T(8,128)(2,1)S(1)}, bf16[256,2048]{1,0:T(8,128)(2,1)S(1)}, u32[]{:S(2)}, u32[]{:S(2)}) collective-permute-start(bf16[256,2048]{1,0:T(8,128)(2,1)S(1)} %copy-done.21), channel_id=1, source_target_pairs={{0,8},{4,12},{8,0},{12,4},{16,24},{20,28},{24,16},{28,20},{1,9},{5... | collective-permute-start | bytes 3145736 | tf_op jit(solution)/shard_map/ppermute | solution.py:33
  130.9 43.6 %collective-permute-start.8 = (bf16[256,2048]{1,0:T(8,128)(2,1)S(1)}, bf16[256,2048]{1,0:T(8,128)(2,1)S(1)}, u32[]{:S(2)}, u32[]{:S(2)}) collective-permute-start(bf16[256,2048]{1,0:T(8,128)(2,1)S(1)} %pad_maximum_fusion.2), channel_id=1, source_target_pairs={{0,4},{4,0},{8,12},{12,8},{16,20},{20,16},{24,28},{28,24},{1,5},{5... | collective-permute-start | bytes 3145736 | tf_op jit(solution)/shard_map/ppermute | solution.py:33
  135.5 37.2 %collective-permute-start.9 = (bf16[256,2048]{1,0:T(8,128)(2,1)S(1)}, bf16[256,2048]{1,0:T(8,128)(2,1)S(1)}, u32[]{:S(2)}, u32[]{:S(2)}) collective-permute-start(bf16[256,2048]{1,0:T(8,128)(2,1)S(1)} %pad_maximum_fusion.2), channel_id=1, source_target_pairs={{0,8},{4,12},{8,0},{12,4},{16,24},{20,28},{24,16},{28,20},{1,9},{5... | collective-permute-start | bytes 3145736 | tf_op jit(solution)/shard_map/ppermute | solution.py:33
  137.1 35.5 %collective-permute-start.11 = (bf16[256,2048]{1,0:T(8,128)(2,1)S(1)}, bf16[256,2048]{1,0:T(8,128)(2,1)S(1)}, u32[]{:S(2)}, u32[]{:S(2)}) collective-permute-start(bf16[256,2048]{1,0:T(8,128)(2,1)S(1)} %pad_maximum_fusion.2), channel_id=1, source_target_pairs={{0,16},{4,20},{8,24},{12,28},{16,0},{20,4},{24,8},{28,12},{1,17},{... | collective-permute-start | bytes 3145736 | tf_op jit(solution)/shard_map/ppermute | solution.py:33
  138.7 30.9 %collective-permute-start.45 = (bf16[128,2048]{1,0:T(8,128)(2,1)S(1)}, bf16[128,2048]{1,0:T(8,128)(2,1)S(1)}, u32[]{:S(2)}, u32[]{:S(2)}) collective-permute-start(bf16[128,2048]{1,0:T(8,128)(2,1)S(1)} %slice.463), channel_id=1, source_target_pairs={{0,8},{4,12},{8,0},{12,4},{16,24},{20,28},{24,16},{28,20},{1,9},{5... | collective-permute-start | bytes 1572872 | tf_op jit(solution)/shard_map/ppermute | solution.py:33
  141.2 30.8 %collective-permute-start.46 = (bf16[128,2048]{1,0:T(8,128)(2,1)S(1)}, bf16[128,2048]{1,0:T(8,128)(2,1)S(1)}, u32[]{:S(2)}, u32[]{:S(2)}) collective-permute-start(bf16[128,2048]{1,0:T(8,128)(2,1)S(1)} %slice.464), channel_id=1, source_target_pairs={{0,16},{4,20},{8,24},{12,28},{16,0},{20,4},{24,8},{28,12},{1,17},{... | collective-permute-start | bytes 1572872 | tf_op jit(solution)/shard_map/ppermute | solution.py:33
  176.4 22.6 %collective-permute-start.10 = (bf16[256,2048]{1,0:T(8,128)(2,1)S(1)}, bf16[256,2048]{1,0:T(8,128)(2,1)S(1)}, u32[]{:S(2)}, u32[]{:S(2)}) collective-permute-start(bf16[256,2048]{1,0:T(8,128)(2,1)S(1)} %collective-permute-done.9), channel_id=1, source_target_pairs={{0,4},{4,0},{8,12},{12,8},{16,20},{20,16},{24,28},{28,24},{1,5},{5... | collective-permute-start | bytes 3145736 | tf_op jit(solution)/shard_map/ppermute | solution.py:33
  276.2 28.0 %collective-permute-start.49 = (bf16[256,2176]{1,0:T(8,128)(2,1)}, bf16[256,2176]{1,0:T(8,128)(2,1)S(1)}, u32[]{:S(2)}, u32[]{:S(2)}) collective-permute-start(bf16[256,2176]{1,0:T(8,128)(2,1)} %get-tuple-element.39), channel_id=1, source_target_pairs={{0,4},{4,0},{8,12},{12,8},{16,20},{20,16},{24,28},{28,24},{1,5},{5... | collective-permute-start | bytes 3342344 | tf_op jit(solution)/shard_map/ppermute | solution.py:33
  276.7 28.1 %collective-permute-start.53 = (bf16[256,2176]{1,0:T(8,128)(2,1)}, bf16[256,2176]{1,0:T(8,128)(2,1)}, u32[]{:S(2)}, u32[]{:S(2)}) collective-permute-start(bf16[256,2176]{1,0:T(8,128)(2,1)} %get-tuple-element.37), channel_id=1, source_target_pairs={{0,4},{4,0},{8,12},{12,8},{16,20},{20,16},{24,28},{28,24},{1,5},{5... | collective-permute-start | bytes 3342344 | tf_op jit(solution)/shard_map/ppermute | solution.py:33
  299.0 60.3 %collective-permute-start.48 = (bf16[256,2176]{1,0:T(8,128)(2,1)}, bf16[256,2176]{1,0:T(8,128)(2,1)}, u32[]{:S(2)}, u32[]{:S(2)}) collective-permute-start(bf16[256,2176]{1,0:T(8,128)(2,1)} %get-tuple-element.36), channel_id=1, source_target_pairs={{0,4},{4,0},{8,12},{12,8},{16,20},{20,16},{24,28},{28,24},{1,5},{5... | collective-permute-start | bytes 3342344 | tf_op jit(solution)/shard_map/ppermute | solution.py:33
  300.4 36.3 %collective-permute-start.24 = (bf16[256,2048]{1,0:T(8,128)(2,1)}, bf16[256,2048]{1,0:T(8,128)(2,1)}, u32[]{:S(2)}, u32[]{:S(2)}) collective-permute-start(bf16[256,2048]{1,0:T(8,128)(2,1)} %get-tuple-element.43), channel_id=1, source_target_pairs={{0,4},{4,0},{8,12},{12,8},{16,20},{20,16},{24,28},{28,24},{1,5},{5... | collective-permute-start | bytes 3145736 | tf_op jit(solution)/shard_map/ppermute | solution.py:33
  309.4 21.3 %collective-permute-start.54 = (bf16[128,2176]{1,0:T(8,128)(2,1)S(1)}, bf16[128,2176]{1,0:T(8,128)(2,1)S(1)}, u32[]{:S(2)}, u32[]{:S(2)}) collective-permute-start(bf16[128,2176]{1,0:T(8,128)(2,1)S(1)} %get-tuple-element.67), channel_id=1, source_target_pairs={{0,8},{4,12},{8,0},{12,4},{16,24},{20,28},{24,16},{28,20},{1,9},{5... | collective-permute-start | bytes 1671176 | tf_op jit(solution)/shard_map/ppermute | solution.py:33
  322.3 35.0 %collective-permute-start.31 = (bf16[256,2048]{1,0:T(8,128)(2,1)S(1)}, bf16[256,2048]{1,0:T(8,128)(2,1)S(1)}, u32[]{:S(2)}, u32[]{:S(2)}) collective-permute-start(bf16[256,2048]{1,0:T(8,128)(2,1)S(1)} %pad_maximum_fusion.5), channel_id=1, source_target_pairs={{0,16},{4,20},{8,24},{12,28},{16,0},{20,4},{24,8},{28,12},{1,17},{... | collective-permute-start | bytes 3145736 | tf_op jit(solution)/shard_map/ppermute | solution.py:33
  330.7 26.7 %collective-permute-start.28 = (bf16[256,2048]{1,0:T(8,128)(2,1)S(1)}, bf16[256,2048]{1,0:T(8,128)(2,1)S(1)}, u32[]{:S(2)}, u32[]{:S(2)}) collective-permute-start(bf16[256,2048]{1,0:T(8,128)(2,1)S(1)} %pad_maximum_fusion.4), channel_id=1, source_target_pairs={{0,8},{4,12},{8,0},{12,4},{16,24},{20,28},{24,16},{28,20},{1,9},{5... | collective-permute-start | bytes 3145736 | tf_op jit(solution)/shard_map/ppermute | solution.py:33
  334.9 44.4 %collective-permute-start.55 = (bf16[256,2176]{1,0:T(8,128)(2,1)S(1)}, bf16[256,2176]{1,0:T(8,128)(2,1)S(1)}, u32[]{:S(2)}, u32[]{:S(2)}) collective-permute-start(bf16[256,2176]{1,0:T(8,128)(2,1)S(1)} %pad_maximum_fusion.1), channel_id=1, source_target_pairs={{0,16},{4,20},{8,24},{12,28},{16,0},{20,4},{24,8},{28,12},{1,17},{... | collective-permute-start | bytes 3342344 | tf_op jit(solution)/shard_map/ppermute | solution.py:33
  336.7 42.6 %collective-permute-start.52 = (bf16[256,2176]{1,0:T(8,128)(2,1)S(1)}, bf16[256,2176]{1,0:T(8,128)(2,1)S(1)}, u32[]{:S(2)}, u32[]{:S(2)}) collective-permute-start(bf16[256,2176]{1,0:T(8,128)(2,1)S(1)} %pad_maximum_fusion), channel_id=1, source_target_pairs={{0,8},{4,12},{8,0},{12,4},{16,24},{20,28},{24,16},{28,20},{1,9},{5... | collective-permute-start | bytes 3342344 | tf_op jit(solution)/shard_map/ppermute | solution.py:33
  415.8 113.6 %collective-permute-start.35 = (bf16[64,2048]{1,0:T(8,128)(2,1)}, bf16[64,2048]{1,0:T(8,128)(2,1)}, u32[]{:S(2)}, u32[]{:S(2)}) collective-permute-start(bf16[64,2048]{1,0:T(8,128)(2,1)} %pad_maximum_fusion.18), channel_id=1, source_target_pairs={{0,3},{1,0},{2,1},{3,2},{4,7},{5,4},{6,5},{7,6},{8,11},{9,8},{10,9... | collective-permute-start | bytes 786440 | tf_op jit(solution)/shard_map/ppermute | solution.py:37
  424.7 44.8 %collective-permute-start.63 = (bf16[64,1024]{1,0:T(8,128)(2,1)S(1)}, bf16[64,1024]{1,0:T(8,128)(2,1)S(1)}, u32[]{:S(2)}, u32[]{:S(2)}) collective-permute-start(bf16[64,1024]{1,0:T(8,128)(2,1)S(1)} %slice.490), channel_id=1, source_target_pairs={{0,3},{1,0},{2,1},{3,2},{4,7},{5,4},{6,5},{7,6},{8,11},{9,8},{10,9... | collective-permute-start | bytes 393224 | tf_op jit(solution)/shard_map/ppermute | solution.py:37
  428.1 41.4 %collective-permute-start.62 = (bf16[64,1024]{1,0:T(8,128)(2,1)S(1)}, bf16[64,1024]{1,0:T(8,128)(2,1)S(1)}, u32[]{:S(2)}, u32[]{:S(2)}) collective-permute-start(bf16[64,1024]{1,0:T(8,128)(2,1)S(1)} %slice.489), channel_id=1, source_target_pairs={{0,1},{1,2},{2,3},{3,0},{4,5},{5,6},{6,7},{7,4},{8,9},{9,10},{10,1... | collective-permute-start | bytes 393224 | tf_op jit(solution)/shard_map/ppermute | solution.py:37
  516.7 87.3 %collective-permute-start.79 = (bf16[256,1280]{1,0:T(8,128)(2,1)}, bf16[256,1280]{1,0:T(8,128)(2,1)}, u32[]{:S(2)}, u32[]{:S(2)}) collective-permute-start(bf16[256,1280]{1,0:T(8,128)(2,1)} %get-tuple-element.104), channel_id=1, source_target_pairs={{0,4},{4,0},{8,12},{12,8},{16,20},{20,16},{24,28},{28,24},{1,5},{5... | collective-permute-start | bytes 1966088 | tf_op jit(solution)/shard_map/ppermute | solution.py:33
  521.8 77.1 %collective-permute-start.80 = (bf16[256,1280]{1,0:T(8,128)(2,1)}, bf16[256,1280]{1,0:T(8,128)(2,1)}, u32[]{:S(2)}, u32[]{:S(2)}) collective-permute-start(bf16[256,1280]{1,0:T(8,128)(2,1)} %get-tuple-element.104), channel_id=1, source_target_pairs={{0,8},{4,12},{8,0},{12,4},{16,24},{20,28},{24,16},{28,20},{1,9},{5... | collective-permute-start | bytes 1966088 | tf_op jit(solution)/shard_map/ppermute | solution.py:33
  527.4 70.4 %collective-permute-start.82 = (bf16[256,1280]{1,0:T(8,128)(2,1)}, bf16[256,1280]{1,0:T(8,128)(2,1)}, u32[]{:S(2)}, u32[]{:S(2)}) collective-permute-start(bf16[256,1280]{1,0:T(8,128)(2,1)} %get-tuple-element.104), channel_id=1, source_target_pairs={{0,16},{4,20},{8,24},{12,28},{16,0},{20,4},{24,8},{28,12},{1,17},{... | collective-permute-start | bytes 1966088 | tf_op jit(solution)/shard_map/ppermute | solution.py:33
  534.3 44.3 %collective-permute-start.36 = (bf16[64,2048]{1,0:T(8,128)(2,1)}, bf16[64,2048]{1,0:T(8,128)(2,1)S(1)}, u32[]{:S(2)}, u32[]{:S(2)}) collective-permute-start(bf16[64,2048]{1,0:T(8,128)(2,1)} %get-tuple-element.107), channel_id=1, source_target_pairs={{0,3},{1,0},{2,1},{3,2},{4,7},{5,4},{6,5},{7,6},{8,11},{9,8},{10,9... | collective-permute-start | bytes 786440 | tf_op jit(solution)/shard_map/ppermute | solution.py:37
  537.0 43.2 %collective-permute-start.37 = (bf16[64,2048]{1,0:T(8,128)(2,1)}, bf16[64,2048]{1,0:T(8,128)(2,1)S(1)}, u32[]{:S(2)}, u32[]{:S(2)}) collective-permute-start(bf16[64,2048]{1,0:T(8,128)(2,1)} %get-tuple-element.107), channel_id=1, source_target_pairs={{0,1},{1,2},{2,3},{3,0},{4,5},{5,6},{6,7},{7,4},{8,9},{9,10},{10,1... | collective-permute-start | bytes 786440 | tf_op jit(solution)/shard_map/ppermute | solution.py:37
  (189 other events, 2418.6 us)
Sparse Core Ops, SparseCore 0:
  416.9 32.4 reduce-scatter.1
where the time goes:
time: 648 us; the launch traced here: 638 us
  waiting for transfers between devices  165 us (25%)
  matrix products  139 us (21%)
  starting transfers between devices  110 us (17%)
  local copies, waits for them, and re-layouts  83.2 us (13%)
  other arithmetic  65 us (10%)
  blocking collectives  58.9 us (9%)
  between operations  16.9 us (3%)
    ppermute x70, waiting for transfers between devices, swap(): return lax.ppermute(value, 'dp', [(i, i ^ bit) for i in range(count)])  104 us
    ppermute x32, starting transfers between devices, shift(): lax.ppermute(value, 'tensor', [(i, (i + step) % count) for i in range(cou...  56.7 us
    unnamed x290, local copies, waits for them, and re-layouts  53.5 us
    ppermute x70, starting transfers between devices, swap(): return lax.ppermute(value, 'dp', [(i, i ^ bit) for i in range(count)])  53.5 us
    ppermute x32, waiting for transfers between devices, shift(): lax.ppermute(value, 'tensor', [(i, (i + step) % count) for i in range(cou...  44.8 us
    dot_general x9, matrix products, dot_nn(): lax.dot_general(a, b, (((1,), (0,)), ((), ())), preferred_element_type=F32)  42.5 us
    psum x1, blocking collectives, local(): gains = lax.psum(gains, ('dp', 'tensor'))  39.3 us
    dot_general x6, matrix products, dot_tn(): lax.dot_general(a, b, (((0,), (0,)), ((), ())), preferred_element_type=F32)  37.1 us
  transfers between devices with their start and end apart: 103, of which 31 were waited for; matrix products, arithmetic and copies ran while one was open for 30% of the time, Pallas kernels for 0%

commit v1 on v0

--- a/solution.py
+++ b/solution.py
@@ -7,6 +7,11 @@
 THETA = 1000000.0
 F32 = jnp.float32
 BF16 = jnp.bfloat16
+
+
+def carry_classes_by_axis(shard_in):
+    taken_in = lax.all_gather(shard_in, axis_name="tensor").sum(axis=0)
+    return taken_in
 
 
 def rms_scale(values):
@@ -316,8 +321,8 @@
     query_weight_grad = qkv_w[:, :q_cols]
     key_weight_grad = qkv_w[:, q_cols : q_cols + kv_cols]
     value_weight_grad = qkv_w[:, q_cols + kv_cols :]
-    router_sum = lax.psum(
-        lax.psum_scatter(router_part.astype(BF16), "dp", scatter_dimension=0, tiled=True), "tensor"
+    router_sum = carry_classes_by_axis(
+        lax.psum_scatter(router_part.astype(BF16), "dp", scatter_dimension=0, tiled=True)
     ).astype(F32)
     gains = jnp.concatenate([attn_gain_part, ffn_gain_part, q_gain_part, k_gain_part])
     gains = lax.psum(gains, ("dp", "tensor"))

time: 648 us -> 642 us (level)
    psum x1 -> x0, blocking collectives: 19.5 us -> none  [local(): lax.psum(lax.psum_scatter(router_part.astype(BF16), 'dp', scatter_dimensi...]
    all_gather x0 -> x1, blocking collectives: none -> 13.5 us  [carry_classes_by_axis(): taken_in = lax.all_gather(shard_in, axis_name='tensor').sum(axis=0)]
  transfers between devices with their start and end apart: 103 -> 103, of which waited for: 31 -> 32; matrix products, arithmetic and copies ran while one was open for 30% -> 30% of each run, Pallas kernels for 0% -> 0%
where the time goes in v1:
time: 642 us; the launch traced here: 632 us
  waiting for transfers between devices  165 us (26%)
  matrix products  139 us (22%)
  starting transfers between devices  110 us (17%)
  local copies, waits for them, and re-layouts  83.2 us (13%)
  other arithmetic  64.9 us (10%)
  blocking collectives  52.6 us (8%)
  between operations  16.9 us (3%)
    ppermute x70, waiting for transfers between devices, swap(): return lax.ppermute(value, 'dp', [(i, i ^ bit) for i in range(count)])  108 us
    ppermute x70, starting transfers between devices, swap(): return lax.ppermute(value, 'dp', [(i, i ^ bit) for i in range(count)])  57.7 us
    unnamed x290, local copies, waits for them, and re-layouts  53.6 us
    ppermute x32, starting transfers between devices, shift(): lax.ppermute(value, 'tensor', [(i, (i + step) % count) for i in range(cou...  52 us
    dot_general x9, matrix products, dot_nn(): lax.dot_general(a, b, (((1,), (0,)), ((), ())), preferred_element_type=F32)  42.5 us
    ppermute x32, waiting for transfers between devices, shift(): lax.ppermute(value, 'tensor', [(i, (i + step) % count) for i in range(cou...  41 us
    psum x1, blocking collectives, local(): gains = lax.psum(gains, ('dp', 'tensor'))  39 us
    dot_general x6, matrix products, dot_tn(): lax.dot_general(a, b, (((0,), (0,)), ((), ())), preferred_element_type=F32)  37.1 us
  transfers between devices with their start and end apart: 103, of which 32 were waited for; matrix products, arithmetic and copies ran while one was open for 30% of the time, Pallas kernels for 0%

profile of v1, /device:TPU:0, one launch (start us, length us, event | category | flops | bytes accessed | tf_op | source)
XLA Modules:
  0.0 631.6 jit_solution(1307401260524298161)
XLA Ops:
  75.1 4.1 collective-permute-done.76
  83.7 6.4 %collective-permute-done.1 = bf16[64,2048]{1,0:T(8,128)(2,1)S(1)} collective-permute-done((bf16[64,2048]{1,0:T(8,128)(2,1)S(1)}, bf16[64,2048]{1,0:T(8,128)(2,1)S(1)}, u32[]{:S(2)}, u32[]{:S(2)}) %collective-permute-start.1) | collective-permute-done | bytes 262176 | tf_op jit(solution)/shard_map/ppermute | solution.py:42
  121.8 9.1 %collective-permute-done.43 = bf16[256,2048]{1,0:T(8,128)(2,1)S(1)} collective-permute-done((bf16[256,2048]{1,0:T(8,128)(2,1)S(1)}, bf16[256,2048]{1,0:T(8,128)(2,1)S(1)}, u32[]{:S(2)}, u32[]{:S(2)}) %collective-permute-start.43) | collective-permute-done | bytes 1048608 | tf_op jit(solution)/shard_map/ppermute | solution.py:38
  144.5 25.2 %collective-permute-done.45 = bf16[128,2048]{1,0:T(8,128)(2,1)S(1)} collective-permute-done((bf16[128,2048]{1,0:T(8,128)(2,1)S(1)}, bf16[128,2048]{1,0:T(8,128)(2,1)S(1)}, u32[]{:S(2)}, u32[]{:S(2)}) %collective-permute-start.45) | collective-permute-done | bytes 524320 | tf_op jit(solution)/shard_map/ppermute | solution.py:38
  181.9 5.3 collective-permute-done.13
  189.9 9.1 %fusion.111 = f32[2048,768]{1,0:T(8,128)S(1)} fusion(bf16[2048,2048]{1,0:T(8,128)(2,1)} %constant_dynamic-update-slice_fusion.21, bf16[768,2048]{1,0:T(8,128)(2,1)S(1)} %bitcast.213), kind=kOutput, calls=%fused_computation.348 | convolution fusion | flops 6442450944 | bytes 17825792 | tf_op jit(solution)/shard_map/dot_general | solution.py:30
  204.4 8.6 %fusion.110 = f32[2048,768]{1,0:T(8,128)} fusion(bf16[2048,2048]{1,0:T(8,128)(2,1)S(1)} %constant_dynamic-update-slice_fusion, bf16[768,2048]{1,0:T(8,128)(2,1)S(1)} %bitcast.211), kind=kOutput, calls=%fused_computation.347 | convolution fusion | flops 6442450944 | bytes 17825792 | tf_op jit(solution)/shard_map/dot_general | solution.py:30
  213.0 8.6 %fusion.109 = f32[2048,768]{1,0:T(8,128)} fusion(bf16[2048,2048]{1,0:T(8,128)(2,1)S(1)} %constant_dynamic-update-slice_fusion, bf16[768,2048]{1,0:T(8,128)(2,1)S(1)} %bitcast.194), kind=kOutput, calls=%fused_computation.346 | convolution fusion | flops 6442450944 | bytes 17825792 | tf_op jit(solution)/shard_map/dot_general | solution.py:30
  221.6 7.6 %fusion.7 = bf16[2048,32]{0,1:T(8,128)(2,1)} fusion(f32[2048,768]{1,0:T(8,128)S(1)} %fusion.111, f32[2048,768]{1,0:T(8,128)S(1)} %copy-done.106, s32[768]{0:T(1024)S(1)} %fusion.79, f32[2048,768]{1,0:T(8,128)} %fusion.109), kind=kOutput, calls=%fused_computation.17 | convolution fusion | flops 613507072 | bytes 19008512 | tf_op jit(solution)/shard_map/dot_general | solution.py:240
  231.2 10.7 %multiply_convert_fusion = (bf16[2048,768]{1,0:T(8,128)(2,1)S(1)}, bf16[2048,768]{1,0:T(8,128)(2,1)S(1)}, bf16[2048,768]{1,0:T(8,128)(2,1)}) fusion(f32[2048,768]{1,0:T(8,128)} %copy-done.105, f32[2048,768]{1,0:T(8,128)} %fusion.109, f32[2048,768]{1,0:T(8,128)} %fusion.110, s32[768]{0:T(1024)S(1)} %fusion.79, f32[2048]{0:T(1024)S(1)} %fusion.76, ...), kind=kOutput, calls=%fused_computation.7 | convolution fusion | flops 631005184 | bytes 28666880 | tf_op jit(solution)/shard_map/dot_general | solution.py:229
  242.0 9.5 %fusion.112 = f32[2048,2048]{1,0:T(8,128)} fusion(bf16[2048,768]{1,0:T(8,128)(2,1)S(1)} %get-tuple-element.34, bf16[768,2048]{1,0:T(8,128)(2,1)S(1)} %bitcast.195), kind=kOutput, calls=%fused_computation.349 | convolution fusion | flops 6442450944 | bytes 23068672 | tf_op jit(solution)/shard_map/dot_general | solution.py:26
  251.5 12.6 %add_convert_fusion = bf16[2048,2048]{1,0:T(8,128)(2,1)} fusion(f32[2048,2048]{1,0:T(8,128)} %fusion.112, bf16[2048,768]{1,0:T(8,128)(2,1)S(1)} %get-tuple-element.33, bf16[768,2048]{1,0:T(8,128)(2,1)S(1)} %bitcast.212), kind=kOutput, calls=%fused_computation.2 | convolution fusion | flops 6450839552 | bytes 31457280 | tf_op jit(solution)/shard_map/dot_general | solution.py:26
  264.0 8.0 %fusion.1 = bf16[2048,2176]{1,0:T(8,128)(2,1)} fusion(bf16[2048,32]{1,0:T(8,128)(2,1)S(1)} %copy-done.26, bf16[2048,2048]{1,0:T(8,128)(2,1)} %add_convert_fusion), kind=kLoop, calls=%fused_computation.3 | loop fusion | flops 26738688 | bytes 17432576 | tf_op jit(solution)/shard_map/concatenate | solution.py:248
  272.0 4.2 fusion.94
  276.7 9.2 %convolution_convert_fusion = bf16[2048,2048]{1,0:T(8,128)(2,1)S(1)} fusion(bf16[2048,768]{1,0:T(8,128)(2,1)} %get-tuple-element.35, bf16[768,2048]{1,0:T(8,128)(2,1)S(1)} %bitcast.214), kind=kOutput, calls=%fused_computation.4 | convolution fusion | flops 6446645248 | bytes 14680064 | tf_op jit(solution)/shard_map/dot_general | solution.py:26
  288.4 10.5 %fusion.116 = f32[768,2048]{1,0:T(8,128)} fusion(bf16[2048,768]{1,0:T(8,128)(2,1)} %copy-done.109, bf16[2048,2048]{1,0:T(8,128)(2,1)S(1)} %bitcast.202), kind=kOutput, calls=%fused_computation.353 | convolution fusion | flops 6442450944 | bytes 17825792 | tf_op jit(solution)/shard_map/dot_general | solution.py:34
  310.9 8.4 %collective-permute-done.30 = bf16[128,2048]{1,0:T(8,128)(2,1)} collective-permute-done((bf16[128,2048]{1,0:T(8,128)(2,1)}, bf16[128,2048]{1,0:T(8,128)(2,1)}, u32[]{:S(2)}, u32[]{:S(2)}) %collective-permute-start.30) | collective-permute-done | bytes 524320 | tf_op jit(solution)/shard_map/ppermute | solution.py:38
  323.0 7.7 %collective-permute-done.54 = bf16[128,2176]{1,0:T(8,128)(2,1)S(1)} collective-permute-done((bf16[128,2176]{1,0:T(8,128)(2,1)S(1)}, bf16[128,2176]{1,0:T(8,128)(2,1)S(1)}, u32[]{:S(2)}, u32[]{:S(2)}) %collective-permute-start.54) | collective-permute-done | bytes 557088 | tf_op jit(solution)/shard_map/ppermute | solution.py:38
  337.4 10.7 %fusion.117 = f32[768,2048]{1,0:T(8,128)} fusion(bf16[2048,768]{1,0:T(8,128)(2,1)} %copy-done.108, bf16[2048,2048]{1,0:T(8,128)(2,1)S(1)} %bitcast.202), kind=kOutput, calls=%fused_computation.354 | convolution fusion | flops 6442450944 | bytes 17825792 | tf_op jit(solution)/shard_map/dot_general | solution.py:34
  348.1 9.2 %collective-permute-done.31 = bf16[256,2048]{1,0:T(8,128)(2,1)S(1)} collective-permute-done((bf16[256,2048]{1,0:T(8,128)(2,1)S(1)}, bf16[256,2048]{1,0:T(8,128)(2,1)S(1)}, u32[]{:S(2)}, u32[]{:S(2)}) %collective-permute-start.31) | collective-permute-done | bytes 1048608 | tf_op jit(solution)/shard_map/ppermute | solution.py:38
  359.3 20.0 %collective-permute-done.55 = bf16[256,2176]{1,0:T(8,128)(2,1)S(1)} collective-permute-done((bf16[256,2176]{1,0:T(8,128)(2,1)S(1)}, bf16[256,2176]{1,0:T(8,128)(2,1)S(1)}, u32[]{:S(2)}, u32[]{:S(2)}) %collective-permute-start.55) | collective-permute-done | bytes 1114144 | tf_op jit(solution)/shard_map/ppermute | solution.py:38
  395.1 11.0 %fusion.118 = f32[768,2048]{1,0:T(8,128)} fusion(bf16[2048,768]{1,0:T(8,128)(2,1)S(1)} %copy-done.107, bf16[2048,2048]{1,0:T(8,128)(2,1)} %constant_dynamic-update-slice_fusion.21), kind=kOutput, calls=%fused_computation.355 | convolution fusion | flops 6442450944 | bytes 17825792 | tf_op jit(solution)/shard_map/dot_general | solution.py:34
  416.8 7.9 %collective-permute-done.60 = bf16[64,2048]{1,0:T(8,128)(2,1)S(1)} collective-permute-done((bf16[64,2048]{1,0:T(8,128)(2,1)S(1)}, bf16[64,2048]{1,0:T(8,128)(2,1)S(1)}, u32[]{:S(2)}, u32[]{:S(2)}) %collective-permute-start.60) | collective-permute-done | bytes 262176 | tf_op jit(solution)/shard_map/ppermute | solution.py:42
  428.1 4.8 collective-permute-start.62
  433.6 15.8 %reduce-scatter.2.cloned.1.call-done = bf16[256,32]{0,1:T(8,128)(2,1)} async-done(((bf16[2048,32]{0,1:T(8,128)(2,1)}), bf16[256,32]{0,1:T(8,128)(2,1)}) %reduce-scatter.2.cloned.1.call-update) | async-done | bytes 16400 | tf_op jit(solution)/shard_map/reduce_scatter | solution.py:325
  449.4 13.5 %all-gather = bf16[1024,32]{0,1:T(8,128)(2,1)S(1)} all-gather(bf16[256,32]{0,1:T(8,128)(2,1)} %reduce-scatter.2.cloned.1.call-done), channel_id=2, replica_groups=mesh['dp'=8,'tensor'=4] {'tensor'}, dimensions={0}, use_global_device_ids=true | all-gather | bytes 81920 | tf_op jit(solution)/shard_map/all_gather | solution.py:13
  505.2 5.1 collective-permute-done.91
  511.9 7.1 %collective-permute-start.80 = (bf16[256,1280]{1,0:T(8,128)(2,1)}, bf16[256,1280]{1,0:T(8,128)(2,1)}, u32[]{:S(2)}, u32[]{:S(2)}) collective-permute-start(bf16[256,1280]{1,0:T(8,128)(2,1)} %get-tuple-element.104), channel_id=1, source_target_pairs={{0,8},{4,12},{8,0},{12,4},{16,24},{20,28},{24,16},{28,20},{1,9},{5... | collective-permute-start | bytes 1966088 | tf_op jit(solution)/shard_map/ppermute | solution.py:38
  533.1 39.0 %psum.7 = f32[4352]{0:T(1024)S(1)} all-reduce(f32[4352]{0:T(1024)S(1)} %pad_maximum_fusion.24), channel_id=1, replica_groups=mesh['dp'=8,'tensor'=4] {'dp','tensor'}, use_global_device_ids=true, to_apply=%region_27.29 | all-reduce | flops 4352 | bytes 34816 | tf_op jit(solution)/shard_map/psum | solution.py:328
  576.9 10.7 %collective-permute-done.69 = bf16[64,2048]{1,0:T(8,128)(2,1)S(1)} collective-permute-done((bf16[64,2048]{1,0:T(8,128)(2,1)S(1)}, bf16[64,2048]{1,0:T(8,128)(2,1)S(1)}, u32[]{:S(2)}, u32[]{:S(2)}) %collective-permute-start.69) | collective-permute-done | bytes 262176 | tf_op jit(solution)/shard_map/ppermute | solution.py:42
  604.4 7.4 %fusion.33 = bf16[256,2048]{1,0:T(8,128)(2,1)} fusion(s32[]{:T(128)S(6)} %select_n.114, bf16[64,2048]{1,0:T(8,128)(2,1)} %get-tuple-element.107, bf16[64,2048]{1,0:T(8,128)(2,1)S(1)} %collective-permute-done.36, bf16[64,1024]{1,0:T(8,128)(2,1)S(1)} %collective-permute-done.38, bf16[64,1024]{1,0:T(8,128)(2,1)S(1)} %collective-permute-done.39, ...), kind=kLoop, calls=%fused_computation.92 | loop fusion | flops 10485760 | bytes 2097156 | tf_op jit(solution)/shard_map/jit(_roll_dynamic)/concatenate | solution.py:114
  612.2 6.5 %fusion.23 = bf16[256,2048]{1,0:T(8,128)(2,1)} fusion(s32[]{:T(128)S(6)} %select_n.114, bf16[64,2048]{1,0:T(8,128)(2,1)S(1)} %get-tuple-element.106, bf16[64,2048]{1,0:T(8,128)(2,1)S(1)} %collective-permute-done.68, bf16[64,1024]{1,0:T(8,128)(2,1)S(1)} %collective-permute-done.70, bf16[64,1024]{1,0:T(8,128)(2,1)S(1)} %collective-permute-done.71, ...), kind=kLoop, calls=%fused_computation.82 | loop fusion | flops 10485760 | bytes 2097156 | tf_op jit(solution)/shard_map/jit(_roll_dynamic)/concatenate | solution.py:114
  (650 shorter events, 281.2 us)
Async XLA Ops:
  7.2 442.2 %reduce-scatter.2.cloned.1.call-start = ((), (), s32[]{:S(2)}) async-start(), calls=%async_computation.1 | async-start | bytes 147456 | tf_op jit(solution)/shard_map/reduce_scatter | solution.py:325
  8.8 44.6 %collective-permute-start.16 = (s32[256,8]{0,1:T(8,128)S(1)}, s32[256,8]{0,1:T(8,128)S(1)}, u32[]{:S(2)}, u32[]{:S(2)}) collective-permute-start(s32[256,8]{0,1:T(8,128)S(1)} %get-tuple-element.28), channel_id=1, source_target_pairs={{0,4},{4,0},{8,12},{12,8},{16,20},{20,16},{24,28},{28,24},{1,5},{5... | collective-permute-start | bytes 24584 | tf_op jit(solution)/shard_map/ppermute | solution.py:38
  9.3 43.6 %collective-permute-start.17 = (s32[256,8]{0,1:T(8,128)S(1)}, s32[256,8]{0,1:T(8,128)S(1)}, u32[]{:S(2)}, u32[]{:S(2)}) collective-permute-start(s32[256,8]{0,1:T(8,128)S(1)} %get-tuple-element.28), channel_id=1, source_target_pairs={{0,8},{4,12},{8,0},{12,4},{16,24},{20,28},{24,16},{28,20},{1,9},{5... | collective-permute-start | bytes 24584 | tf_op jit(solution)/shard_map/ppermute | solution.py:38
  11.8 38.7 %collective-permute-start.19 = (s32[256,8]{0,1:T(8,128)S(1)}, s32[256,8]{0,1:T(8,128)S(1)}, u32[]{:S(2)}, u32[]{:S(2)}) collective-permute-start(s32[256,8]{0,1:T(8,128)S(1)} %get-tuple-element.28), channel_id=1, source_target_pairs={{0,16},{4,20},{8,24},{12,28},{16,0},{20,4},{24,8},{28,12},{1,17},{... | collective-permute-start | bytes 24584 | tf_op jit(solution)/shard_map/ppermute | solution.py:38
  31.7 68.2 %collective-permute-start.94 = (bf16[256,1024]{0,1:T(8,128)(2,1)}, bf16[256,1024]{0,1:T(8,128)(2,1)}, u32[]{:S(2)}, u32[]{:S(2)}) collective-permute-start(bf16[256,1024]{0,1:T(8,128)(2,1)} %bitcast.11), channel_id=1, source_target_pairs={{0,4},{4,0},{8,12},{12,8},{16,20},{20,16},{24,28},{28,24},{1,5},{5... | collective-permute-start | bytes 1572872 | tf_op jit(solution)/shard_map/ppermute | solution.py:38
  37.2 27.6 %collective-permute-start = (bf16[64,1024]{1,0:T(8,128)(2,1)}, bf16[64,1024]{1,0:T(8,128)(2,1)}, u32[]{:S(2)}, u32[]{:S(2)}) collective-permute-start(bf16[64,1024]{1,0:T(8,128)(2,1)} %get-tuple-element.100), channel_id=1, source_target_pairs={{0,1},{1,2},{2,3},{3,0},{4,5},{5,6},{6,7},{7,4},{8,9},{9,10},{10,1... | collective-permute-start | bytes 393224 | tf_op jit(solution)/shard_map/ppermute | solution.py:42
  96.8 34.2 %collective-permute-start.40 = (bf16[256,2048]{1,0:T(8,128)(2,1)}, bf16[256,2048]{1,0:T(8,128)(2,1)S(1)}, u32[]{:S(2)}, u32[]{:S(2)}) collective-permute-start(bf16[256,2048]{1,0:T(8,128)(2,1)} %get-tuple-element.22), channel_id=1, source_target_pairs={{0,4},{4,0},{8,12},{12,8},{16,20},{20,16},{24,28},{28,24},{1,5},{5... | collective-permute-start | bytes 3145736 | tf_op jit(solution)/shard_map/ppermute | solution.py:38
  106.4 24.5 %collective-permute-start.43 = (bf16[256,2048]{1,0:T(8,128)(2,1)S(1)}, bf16[256,2048]{1,0:T(8,128)(2,1)S(1)}, u32[]{:S(2)}, u32[]{:S(2)}) collective-permute-start(bf16[256,2048]{1,0:T(8,128)(2,1)S(1)} %copy-done.21), channel_id=1, source_target_pairs={{0,16},{4,20},{8,24},{12,28},{16,0},{20,4},{24,8},{28,12},{1,17},{... | collective-permute-start | bytes 3145736 | tf_op jit(solution)/shard_map/ppermute | solution.py:38
  111.7 23.8 %collective-permute-start.41 = (bf16[256,2048]{1,0:T(8,128)(2,1)S(1)}, bf16[256,2048]{1,0:T(8,128)(2,1)S(1)}, u32[]{:S(2)}, u32[]{:S(2)}) collective-permute-start(bf16[256,2048]{1,0:T(8,128)(2,1)S(1)} %copy-done.21), channel_id=1, source_target_pairs={{0,8},{4,12},{8,0},{12,4},{16,24},{20,28},{24,16},{28,20},{1,9},{5... | collective-permute-start | bytes 3145736 | tf_op jit(solution)/shard_map/ppermute | solution.py:38
  130.9 43.6 %collective-permute-start.8 = (bf16[256,2048]{1,0:T(8,128)(2,1)S(1)}, bf16[256,2048]{1,0:T(8,128)(2,1)S(1)}, u32[]{:S(2)}, u32[]{:S(2)}) collective-permute-start(bf16[256,2048]{1,0:T(8,128)(2,1)S(1)} %pad_maximum_fusion.2), channel_id=1, source_target_pairs={{0,4},{4,0},{8,12},{12,8},{16,20},{20,16},{24,28},{28,24},{1,5},{5... | collective-permute-start | bytes 3145736 | tf_op jit(solution)/shard_map/ppermute | solution.py:38
  135.5 37.2 %collective-permute-start.9 = (bf16[256,2048]{1,0:T(8,128)(2,1)S(1)}, bf16[256,2048]{1,0:T(8,128)(2,1)S(1)}, u32[]{:S(2)}, u32[]{:S(2)}) collective-permute-start(bf16[256,2048]{1,0:T(8,128)(2,1)S(1)} %pad_maximum_fusion.2), channel_id=1, source_target_pairs={{0,8},{4,12},{8,0},{12,4},{16,24},{20,28},{24,16},{28,20},{1,9},{5... | collective-permute-start | bytes 3145736 | tf_op jit(solution)/shard_map/ppermute | solution.py:38
  137.1 35.5 %collective-permute-start.11 = (bf16[256,2048]{1,0:T(8,128)(2,1)S(1)}, bf16[256,2048]{1,0:T(8,128)(2,1)S(1)}, u32[]{:S(2)}, u32[]{:S(2)}) collective-permute-start(bf16[256,2048]{1,0:T(8,128)(2,1)S(1)} %pad_maximum_fusion.2), channel_id=1, source_target_pairs={{0,16},{4,20},{8,24},{12,28},{16,0},{20,4},{24,8},{28,12},{1,17},{... | collective-permute-start | bytes 3145736 | tf_op jit(solution)/shard_map/ppermute | solution.py:38
  138.7 30.9 %collective-permute-start.45 = (bf16[128,2048]{1,0:T(8,128)(2,1)S(1)}, bf16[128,2048]{1,0:T(8,128)(2,1)S(1)}, u32[]{:S(2)}, u32[]{:S(2)}) collective-permute-start(bf16[128,2048]{1,0:T(8,128)(2,1)S(1)} %slice.463), channel_id=1, source_target_pairs={{0,8},{4,12},{8,0},{12,4},{16,24},{20,28},{24,16},{28,20},{1,9},{5... | collective-permute-start | bytes 1572872 | tf_op jit(solution)/shard_map/ppermute | solution.py:38
  141.2 30.8 %collective-permute-start.46 = (bf16[128,2048]{1,0:T(8,128)(2,1)S(1)}, bf16[128,2048]{1,0:T(8,128)(2,1)S(1)}, u32[]{:S(2)}, u32[]{:S(2)}) collective-permute-start(bf16[128,2048]{1,0:T(8,128)(2,1)S(1)} %slice.464), channel_id=1, source_target_pairs={{0,16},{4,20},{8,24},{12,28},{16,0},{20,4},{24,8},{28,12},{1,17},{... | collective-permute-start | bytes 1572872 | tf_op jit(solution)/shard_map/ppermute | solution.py:38
  176.4 22.6 %collective-permute-start.10 = (bf16[256,2048]{1,0:T(8,128)(2,1)S(1)}, bf16[256,2048]{1,0:T(8,128)(2,1)S(1)}, u32[]{:S(2)}, u32[]{:S(2)}) collective-permute-start(bf16[256,2048]{1,0:T(8,128)(2,1)S(1)} %collective-permute-done.9), channel_id=1, source_target_pairs={{0,4},{4,0},{8,12},{12,8},{16,20},{20,16},{24,28},{28,24},{1,5},{5... | collective-permute-start | bytes 3145736 | tf_op jit(solution)/shard_map/ppermute | solution.py:38
  276.2 28.0 %collective-permute-start.49 = (bf16[256,2176]{1,0:T(8,128)(2,1)}, bf16[256,2176]{1,0:T(8,128)(2,1)S(1)}, u32[]{:S(2)}, u32[]{:S(2)}) collective-permute-start(bf16[256,2176]{1,0:T(8,128)(2,1)} %get-tuple-element.39), channel_id=1, source_target_pairs={{0,4},{4,0},{8,12},{12,8},{16,20},{20,16},{24,28},{28,24},{1,5},{5... | collective-permute-start | bytes 3342344 | tf_op jit(solution)/shard_map/ppermute | solution.py:38
  276.7 28.1 %collective-permute-start.53 = (bf16[256,2176]{1,0:T(8,128)(2,1)}, bf16[256,2176]{1,0:T(8,128)(2,1)}, u32[]{:S(2)}, u32[]{:S(2)}) collective-permute-start(bf16[256,2176]{1,0:T(8,128)(2,1)} %get-tuple-element.37), channel_id=1, source_target_pairs={{0,4},{4,0},{8,12},{12,8},{16,20},{20,16},{24,28},{28,24},{1,5},{5... | collective-permute-start | bytes 3342344 | tf_op jit(solution)/shard_map/ppermute | solution.py:38
  299.0 60.3 %collective-permute-start.48 = (bf16[256,2176]{1,0:T(8,128)(2,1)}, bf16[256,2176]{1,0:T(8,128)(2,1)}, u32[]{:S(2)}, u32[]{:S(2)}) collective-permute-start(bf16[256,2176]{1,0:T(8,128)(2,1)} %get-tuple-element.36), channel_id=1, source_target_pairs={{0,4},{4,0},{8,12},{12,8},{16,20},{20,16},{24,28},{28,24},{1,5},{5... | collective-permute-start | bytes 3342344 | tf_op jit(solution)/shard_map/ppermute | solution.py:38
  300.4 36.3 %collective-permute-start.24 = (bf16[256,2048]{1,0:T(8,128)(2,1)}, bf16[256,2048]{1,0:T(8,128)(2,1)}, u32[]{:S(2)}, u32[]{:S(2)}) collective-permute-start(bf16[256,2048]{1,0:T(8,128)(2,1)} %get-tuple-element.43), channel_id=1, source_target_pairs={{0,4},{4,0},{8,12},{12,8},{16,20},{20,16},{24,28},{28,24},{1,5},{5... | collective-permute-start | bytes 3145736 | tf_op jit(solution)/shard_map/ppermute | solution.py:38
  309.4 21.3 %collective-permute-start.54 = (bf16[128,2176]{1,0:T(8,128)(2,1)S(1)}, bf16[128,2176]{1,0:T(8,128)(2,1)S(1)}, u32[]{:S(2)}, u32[]{:S(2)}) collective-permute-start(bf16[128,2176]{1,0:T(8,128)(2,1)S(1)} %get-tuple-element.67), channel_id=1, source_target_pairs={{0,8},{4,12},{8,0},{12,4},{16,24},{20,28},{24,16},{28,20},{1,9},{5... | collective-permute-start | bytes 1671176 | tf_op jit(solution)/shard_map/ppermute | solution.py:38
  322.3 35.0 %collective-permute-start.31 = (bf16[256,2048]{1,0:T(8,128)(2,1)S(1)}, bf16[256,2048]{1,0:T(8,128)(2,1)S(1)}, u32[]{:S(2)}, u32[]{:S(2)}) collective-permute-start(bf16[256,2048]{1,0:T(8,128)(2,1)S(1)} %pad_maximum_fusion.5), channel_id=1, source_target_pairs={{0,16},{4,20},{8,24},{12,28},{16,0},{20,4},{24,8},{28,12},{1,17},{... | collective-permute-start | bytes 3145736 | tf_op jit(solution)/shard_map/ppermute | solution.py:38
  330.7 26.7 %collective-permute-start.28 = (bf16[256,2048]{1,0:T(8,128)(2,1)S(1)}, bf16[256,2048]{1,0:T(8,128)(2,1)S(1)}, u32[]{:S(2)}, u32[]{:S(2)}) collective-permute-start(bf16[256,2048]{1,0:T(8,128)(2,1)S(1)} %pad_maximum_fusion.4), channel_id=1, source_target_pairs={{0,8},{4,12},{8,0},{12,4},{16,24},{20,28},{24,16},{28,20},{1,9},{5... | collective-permute-start | bytes 3145736 | tf_op jit(solution)/shard_map/ppermute | solution.py:38
  334.9 44.4 %collective-permute-start.55 = (bf16[256,2176]{1,0:T(8,128)(2,1)S(1)}, bf16[256,2176]{1,0:T(8,128)(2,1)S(1)}, u32[]{:S(2)}, u32[]{:S(2)}) collective-permute-start(bf16[256,2176]{1,0:T(8,128)(2,1)S(1)} %pad_maximum_fusion.1), channel_id=1, source_target_pairs={{0,16},{4,20},{8,24},{12,28},{16,0},{20,4},{24,8},{28,12},{1,17},{... | collective-permute-start | bytes 3342344 | tf_op jit(solution)/shard_map/ppermute | solution.py:38
  336.7 42.6 %collective-permute-start.52 = (bf16[256,2176]{1,0:T(8,128)(2,1)S(1)}, bf16[256,2176]{1,0:T(8,128)(2,1)S(1)}, u32[]{:S(2)}, u32[]{:S(2)}) collective-permute-start(bf16[256,2176]{1,0:T(8,128)(2,1)S(1)} %pad_maximum_fusion), channel_id=1, source_target_pairs={{0,8},{4,12},{8,0},{12,4},{16,24},{20,28},{24,16},{28,20},{1,9},{5... | collective-permute-start | bytes 3342344 | tf_op jit(solution)/shard_map/ppermute | solution.py:38
  415.8 107.9 %collective-permute-start.35 = (bf16[64,2048]{1,0:T(8,128)(2,1)}, bf16[64,2048]{1,0:T(8,128)(2,1)}, u32[]{:S(2)}, u32[]{:S(2)}) collective-permute-start(bf16[64,2048]{1,0:T(8,128)(2,1)} %pad_maximum_fusion.18), channel_id=1, source_target_pairs={{0,3},{1,0},{2,1},{3,2},{4,7},{5,4},{6,5},{7,6},{8,11},{9,8},{10,9... | collective-permute-start | bytes 786440 | tf_op jit(solution)/shard_map/ppermute | solution.py:42
  424.7 39.0 %collective-permute-start.63 = (bf16[64,1024]{1,0:T(8,128)(2,1)S(1)}, bf16[64,1024]{1,0:T(8,128)(2,1)S(1)}, u32[]{:S(2)}, u32[]{:S(2)}) collective-permute-start(bf16[64,1024]{1,0:T(8,128)(2,1)S(1)} %slice.490), channel_id=1, source_target_pairs={{0,3},{1,0},{2,1},{3,2},{4,7},{5,4},{6,5},{7,6},{8,11},{9,8},{10,9... | collective-permute-start | bytes 393224 | tf_op jit(solution)/shard_map/ppermute | solution.py:42
  428.1 35.6 %collective-permute-start.62 = (bf16[64,1024]{1,0:T(8,128)(2,1)S(1)}, bf16[64,1024]{1,0:T(8,128)(2,1)S(1)}, u32[]{:S(2)}, u32[]{:S(2)}) collective-permute-start(bf16[64,1024]{1,0:T(8,128)(2,1)S(1)} %slice.489), channel_id=1, source_target_pairs={{0,1},{1,2},{2,3},{3,0},{4,5},{5,6},{6,7},{7,4},{8,9},{9,10},{10,1... | collective-permute-start | bytes 393224 | tf_op jit(solution)/shard_map/ppermute | solution.py:42
  510.9 86.7 %collective-permute-start.79 = (bf16[256,1280]{1,0:T(8,128)(2,1)}, bf16[256,1280]{1,0:T(8,128)(2,1)}, u32[]{:S(2)}, u32[]{:S(2)}) collective-permute-start(bf16[256,1280]{1,0:T(8,128)(2,1)} %get-tuple-element.104), channel_id=1, source_target_pairs={{0,4},{4,0},{8,12},{12,8},{16,20},{20,16},{24,28},{28,24},{1,5},{5... | collective-permute-start | bytes 1966088 | tf_op jit(solution)/shard_map/ppermute | solution.py:38
  511.9 80.7 %collective-permute-start.80 = (bf16[256,1280]{1,0:T(8,128)(2,1)}, bf16[256,1280]{1,0:T(8,128)(2,1)}, u32[]{:S(2)}, u32[]{:S(2)}) collective-permute-start(bf16[256,1280]{1,0:T(8,128)(2,1)} %get-tuple-element.104), channel_id=1, source_target_pairs={{0,8},{4,12},{8,0},{12,4},{16,24},{20,28},{24,16},{28,20},{1,9},{5... | collective-permute-start | bytes 1966088 | tf_op jit(solution)/shard_map/ppermute | solution.py:38
  521.3 70.1 %collective-permute-start.82 = (bf16[256,1280]{1,0:T(8,128)(2,1)}, bf16[256,1280]{1,0:T(8,128)(2,1)}, u32[]{:S(2)}, u32[]{:S(2)}) collective-permute-start(bf16[256,1280]{1,0:T(8,128)(2,1)} %get-tuple-element.104), channel_id=1, source_target_pairs={{0,16},{4,20},{8,24},{12,28},{16,0},{20,4},{24,8},{28,12},{1,17},{... | collective-permute-start | bytes 1966088 | tf_op jit(solution)/shard_map/ppermute | solution.py:38
  528.7 43.4 %collective-permute-start.36 = (bf16[64,2048]{1,0:T(8,128)(2,1)}, bf16[64,2048]{1,0:T(8,128)(2,1)S(1)}, u32[]{:S(2)}, u32[]{:S(2)}) collective-permute-start(bf16[64,2048]{1,0:T(8,128)(2,1)} %get-tuple-element.107), channel_id=1, source_target_pairs={{0,3},{1,0},{2,1},{3,2},{4,7},{5,4},{6,5},{7,6},{8,11},{9,8},{10,9... | collective-permute-start | bytes 786440 | tf_op jit(solution)/shard_map/ppermute | solution.py:42
  528.8 44.9 %collective-permute-start.37 = (bf16[64,2048]{1,0:T(8,128)(2,1)}, bf16[64,2048]{1,0:T(8,128)(2,1)S(1)}, u32[]{:S(2)}, u32[]{:S(2)}) collective-permute-start(bf16[64,2048]{1,0:T(8,128)(2,1)} %get-tuple-element.107), channel_id=1, source_target_pairs={{0,1},{1,2},{2,3},{3,0},{4,5},{5,6},{6,7},{7,4},{8,9},{9,10},{10,1... | collective-permute-start | bytes 786440 | tf_op jit(solution)/shard_map/ppermute | solution.py:42
  (189 other events, 2387.7 us)
Sparse Core Ops, SparseCore 0:
  416.9 32.4 reduce-scatter.1
